TPU v7x, 32 devices: a whole 2x2x4 slice. The times are simulated.
32 devices in a mesh: dp: 8 (over z, x), head: 4 (over y, core).
Axes of the slice: x: 2, y: 2, z: 4, core: 2. Of those that a mesh axis runs over, the one named last changes fastest.
Arguments:
- hidden_in: bfloat16 [8192, 2048], P(('dp', 'head')), may hold values from -6 to 6
- in_gain: float32 [2048], replicated, may hold values from 0.1 to 1.9
- gate_proj: bfloat16 [2048, 4096], P(None, 'head'), may hold values from -0.125 to 0.125
- value_proj: bfloat16 [2048, 4096], P(None, 'head'), may hold values from -0.125 to 0.125
- state_proj: bfloat16 [2048, 256], replicated, may hold values from -0.125 to 0.125
- step_proj: bfloat16 [2048, 64], P(None, 'head'), may hold values from -0.03125 to 0.03125
- conv_value: float32 [4, 4096], P(None, 'head'), may hold values from -3 to 3
- conv_value_bias: float32 [4096], P('head'), may hold values from -3 to 3
- conv_state: float32 [4, 256], replicated, may hold values from -3 to 3
- conv_state_bias: float32 [256], replicated, may hold values from -3 to 3
- step_bias: float32 [64], P('head'), may hold values from -6 to -1
- decay_log: float32 [64], P('head'), may hold values from 0 to 2.77
- skip_gain: float32 [64], P('head'), may hold values from 0.5 to 1.5
- out_gain: float32 [4096], P('head'), may hold values from 0.1 to 1.9
- out_proj: bfloat16 [4096, 2048], P('head'), may hold values from -0.125 to 0.125
- cotangent: bfloat16 [8192, 2048], P(('dp', 'head')), may hold values from -6 to 6
- width_level: int32 [8], P('dp'), may hold values from 0 to 3
Outputs:
- block_out: bfloat16 [8192, 2048], P(('dp', 'head'))
- in_grad: float32 [8192, 2048], P(('dp', 'head'))
- in_gain_grad: float32 [2048], replicated
- gate_proj_grad: float32 [2048, 4096], P('dp', 'head')
- value_proj_grad: float32 [2048, 4096], P('dp', 'head')
- state_proj_grad: float32 [2048, 256], P('dp')
- step_proj_grad: float32 [2048, 64], P('dp', 'head')
- conv_value_grad: float32 [4, 4096], P(None, 'head')
- conv_value_bias_grad: float32 [4096], P('head')
- conv_state_grad: float32 [4, 256], replicated
- conv_state_bias_grad: float32 [256], replicated
- step_bias_grad: float32 [64], P('head')
- decay_log_grad: float32 [64], P('head')
- skip_gain_grad: float32 [64], P('head')
- out_gain_grad: float32 [4096], P('head')
- out_proj_grad: float32 [4096, 2048], P('head', 'dp')
All inputs are finite; a program needn't handle non-finite values.
Results may differ from a plain program's by a relative error of at most 0.0079.
Values may be sent and summed in bfloat16 or wider, within the bound.
A program may use at most 192 MiB of HBM per device.

v0:
```python
import jax
import jax.numpy as jnp
from jax import lax
from jax.sharding import PartitionSpec as P

SPAN = 256
HIGH = lax.Precision.HIGHEST
EPS = 1e-05


def conv_causal(series, kernel, shift):
    kernel_len = kernel.shape[0]
    length = series.shape[0]
    padded = jnp.pad(series, ((kernel_len - 1, 0), (0, 0)))
    running = shift[None, :] + kernel[0][None, :] * padded[0:length]
    for offset in range(1, kernel_len):
        running = running + kernel[offset][None, :] * padded[offset : offset + length]
    return running


def state_space(inputs, step_size, decay_rate, key_rows, query_rows, skip_gain):
    seq_len, heads, head_dim = inputs.shape
    blocks = seq_len // SPAN
    values = inputs.reshape(blocks, SPAN, heads, head_dim)
    deltas = step_size.reshape(blocks, SPAN, heads)
    keys = key_rows.reshape(blocks, SPAN, -1)
    queries = query_rows.reshape(blocks, SPAN, -1)
    cumul = jnp.cumsum(deltas * decay_rate[None, None, :], axis=1)
    inner = jnp.einsum("cin,cjn->cij", queries, keys, precision=HIGH)
    lower = (jnp.arange(SPAN)[:, None] >= jnp.arange(SPAN)[None, :])[None, :, :, None]
    spread = cumul[:, :, None, :] - cumul[:, None, :, :]
    mixing = jnp.where(lower, jnp.exp(jnp.where(lower, spread, 0.0)), 0.0) * inner[:, :, :, None]
    scaled = values * deltas[:, :, :, None]
    within = jnp.einsum("cijh,cjhp->cihp", mixing, scaled, precision=HIGH)
    tails = jnp.exp(cumul[:, -1:, :] - cumul)
    states = jnp.einsum("cjhp,cjn->chpn", scaled * tails[:, :, :, None], keys, precision=HIGH)
    totals = jnp.exp(cumul[:, -1, :])

    def carry_state(state, item):
        fresh, factor = item
        return (factor[:, None, None] * state + fresh, state)

    start = jnp.zeros((heads, head_dim, keys.shape[2]), dtype=inputs.dtype)
    _, entering = lax.scan(carry_state, start, (states, totals))
    across = (
        jnp.einsum("cin,chpn->cihp", queries, entering, precision=HIGH)
        * jnp.exp(cumul)[:, :, :, None]
    )
    result = within + across + values * skip_gain[None, None, :, None]
    return result.reshape(seq_len, heads, head_dim)


def mix_block(
    value_pre,
    state_pre,
    step_pre,
    gate_pre,
    conv_value,
    conv_value_bias,
    conv_state,
    conv_state_bias,
    step_bias,
    decay_log,
    skip_gain,
    keep,
):
    seq_len = value_pre.shape[0]
    heads = step_pre.shape[1]
    value_act = jax.nn.silu(conv_causal(value_pre, conv_value, conv_value_bias))
    state_act = jax.nn.silu(conv_causal(state_pre, conv_state, conv_state_bias))
    half = state_act.shape[1] // 2
    step_size = jax.nn.softplus(step_pre + step_bias[None, :])
    inputs = value_act.reshape(seq_len, heads, -1) * keep[None, :, None]
    result = state_space(
        inputs, step_size, -jnp.exp(decay_log), state_act[:, :half], state_act[:, half:], skip_gain
    )
    return result.reshape(seq_len, -1) * jax.nn.silu(gate_pre)


def contract_rows(left, right):
    return lax.dot_general(
        left, right, (((0,), (0,)), ((), ())), preferred_element_type=jnp.float32
    )


def contract_cols(left, right):
    return lax.dot_general(
        left, right, (((1,), (1,)), ((), ())), preferred_element_type=jnp.float32
    )


def per_device(
    hidden_in,
    in_gain,
    gate_proj,
    value_proj,
    state_proj,
    step_proj,
    conv_value,
    conv_value_bias,
    conv_state,
    conv_state_bias,
    step_bias,
    decay_log,
    skip_gain,
    out_gain,
    out_proj,
    cotangent,
    width_level,
):
    heads_here = step_bias.shape[0]
    head_dim = conv_value.shape[1] // heads_here
    groups = lax.axis_size("head")
    rank = lax.axis_index("head")
    rows_own = hidden_in.shape[0]
    seqs = width_level.shape[0]
    resid = hidden_in.astype(jnp.float32)
    in_scale = lax.rsqrt(jnp.mean(resid * resid, axis=-1, keepdims=True) + EPS)
    normed = (resid * in_scale * in_gain).astype(jnp.bfloat16)
    whole = lax.all_gather(normed, "head", axis=0, tiled=True)
    rows_all = whole.shape[0]
    seq_len = rows_all // seqs
    gate_pre = jnp.dot(whole, gate_proj, preferred_element_type=jnp.float32)
    value_pre = jnp.dot(whole, value_proj, preferred_element_type=jnp.float32)
    state_pre = jnp.dot(whole, state_proj, preferred_element_type=jnp.float32)
    step_pre = jnp.dot(whole, step_proj, preferred_element_type=jnp.float32)
    active = jnp.right_shift(heads_here, 3 - width_level)
    keep = (jnp.arange(heads_here)[None, :] < active[:, None]).astype(jnp.float32)
    seq_count = (active * groups * head_dim).astype(jnp.float32)
    token_count = jnp.broadcast_to(seq_count[:, None], (seqs, seq_len)).reshape(rows_all)
    params = (
        conv_value,
        conv_value_bias,
        conv_state,
        conv_state_bias,
        step_bias,
        decay_log,
        skip_gain,
    )

    def group_mix(value_in, state_in, step_in, gate_in, *weights):

        def split(array):
            return array.reshape(seqs, seq_len, array.shape[1])

        mapped = jax.vmap(
            mix_block, in_axes=(0, 0, 0, 0, None, None, None, None, None, None, None, 0)
        )
        result = mapped(
            split(value_in), split(state_in), split(step_in), split(gate_in), *weights, keep
        )
        return result.reshape(rows_all, -1)

    gated = group_mix(value_pre, state_pre, step_pre, gate_pre, *params)
    squares = lax.psum(jnp.sum(gated * gated, axis=-1), "head")
    out_scale = lax.rsqrt(squares / token_count + EPS)[:, None]
    normed_out = (gated * out_scale * out_gain).astype(jnp.bfloat16)
    own_out = lax.psum_scatter(
        jnp.dot(normed_out, out_proj, preferred_element_type=jnp.float32),
        "head",
        scatter_dimension=0,
        tiled=True,
    )
    block_out = (resid + own_out).astype(jnp.bfloat16)
    cot_all = lax.all_gather(cotangent, "head", axis=0, tiled=True)
    out_proj_part = contract_rows(normed_out, cot_all)
    d_normed_out = contract_cols(cot_all, out_proj)
    weighted = d_normed_out * out_gain
    stat = lax.psum(jnp.sum(weighted * gated, axis=-1), "head")
    d_gated = weighted * out_scale - gated * out_scale**3 * (stat / token_count)[:, None]
    out_gain_part = jnp.sum(d_normed_out * gated * out_scale, axis=0)
    _, pull = jax.vjp(group_mix, value_pre, state_pre, step_pre, gate_pre, *params)
    (
        d_value_pre,
        d_state_pre,
        d_step_pre,
        d_gate_pre,
        g_conv_value,
        g_conv_value_bias,
        g_conv_state,
        g_conv_state_bias,
        g_step_bias,
        g_decay_log,
        g_skip_gain,
    ) = pull(d_gated)
    d_state_pre, g_conv_state, g_conv_state_bias = lax.psum(
        (d_state_pre, g_conv_state, g_conv_state_bias), "head"
    )
    d_gate_low = d_gate_pre.astype(jnp.bfloat16)
    d_value_low = d_value_pre.astype(jnp.bfloat16)
    d_state_low = d_state_pre.astype(jnp.bfloat16)
    d_step_low = d_step_pre.astype(jnp.bfloat16)
    d_normed = lax.psum_scatter(
        contract_cols(d_gate_low, gate_proj)
        + contract_cols(d_value_low, value_proj)
        + contract_cols(d_step_low, step_proj),
        "head",
        scatter_dimension=0,
        tiled=True,
    )
    state_own = lax.dynamic_slice_in_dim(d_state_low, rank * rows_own, rows_own, 0)
    d_normed = d_normed + contract_cols(state_own, state_proj)
    gate_part = contract_rows(whole, d_gate_low)
    value_part = contract_rows(whole, d_value_low)
    state_part = contract_rows(whole, d_state_low)
    step_part = contract_rows(whole, d_step_low)
    scaled_grad = d_normed * in_gain
    in_grad = (
        cotangent.astype(jnp.float32)
        + scaled_grad * in_scale
        - resid
        * in_scale**3
        * jnp.sum(scaled_grad * resid, axis=-1, keepdims=True)
        / resid.shape[1]
    )
    in_gain_grad = lax.psum(jnp.sum(d_normed * resid * in_scale, axis=0), ("dp", "head"))
    (
        conv_value_grad,
        conv_value_bias_grad,
        step_bias_grad,
        decay_log_grad,
        skip_gain_grad,
        out_gain_grad,
        conv_state_grad,
        conv_state_bias_grad,
    ) = lax.psum(
        (
            g_conv_value,
            g_conv_value_bias,
            g_step_bias,
            g_decay_log,
            g_skip_gain,
            out_gain_part,
            g_conv_state,
            g_conv_state_bias,
        ),
        "dp",
    )
    gate_proj_grad, value_proj_grad, state_proj_grad, step_proj_grad, out_proj_grad = (
        lax.psum_scatter(gate_part, "dp", scatter_dimension=0, tiled=True),
        lax.psum_scatter(value_part, "dp", scatter_dimension=0, tiled=True),
        lax.psum_scatter(state_part, "dp", scatter_dimension=0, tiled=True),
        lax.psum_scatter(step_part, "dp", scatter_dimension=0, tiled=True),
        lax.psum_scatter(out_proj_part, "dp", scatter_dimension=1, tiled=True),
    )
    return (
        block_out,
        in_grad,
        in_gain_grad,
        gate_proj_grad,
        value_proj_grad,
        state_proj_grad,
        step_proj_grad,
        conv_value_grad,
        conv_value_bias_grad,
        conv_state_grad,
        conv_state_bias_grad,
        step_bias_grad,
        decay_log_grad,
        skip_gain_grad,
        out_gain_grad,
        out_proj_grad,
    )


def solution(mesh):
    placed = (
        P(("dp", "head"), None),
        P(),
        P(None, "head"),
        P(None, "head"),
        P(),
        P(None, "head"),
        P(None, "head"),
        P("head"),
        P(),
        P(),
        P("head"),
        P("head"),
        P("head"),
        P("head"),
        P("head", None),
        P(("dp", "head"), None),
        P("dp"),
    )
    return jax.shard_map(
        per_device,
        mesh=mesh,
        in_specs=placed,
        out_specs=(
            P(("dp", "head"), None),
            P(("dp", "head"), None),
            P(),
            P("dp", "head"),
            P("dp", "head"),
            P("dp", None),
            P("dp", "head"),
            P(None, "head"),
            P("head"),
            P(),
            P(),
            P("head"),
            P("head"),
            P("head"),
            P("head"),
            P("head", "dp"),
        ),
        check_vma=False,
    )
```

profile of v0, /device:TPU:0, one launch (start us, length us, event | category | flops | bytes accessed | tf_op | source)
XLA Modules:
  0.0 1183.8 jit_solution(4698405417298480208)
XLA Ops:
  15.4 33.9 %all-gather.3.cloned.1.call-done = bf16[1024,2048]{1,0:T(8,128)(2,1)} async-done(((bf16[256,2048]{1,0:T(8,128)(2,1)}), bf16[1024,2048]{1,0:T(8,128)(2,1)}) %all-gather.3.cloned.1.call-update) | async-done | bytes 4194320 | tf_op jit(solution)/shard_map/all_gather | solution.py:120
  114.1 20.4 %fusion.9 = f32[4,16,64,256]{3,2,1,0:T(8,128)} fusion(f32[4,256,256]{2,1,0:T(8,128)S(1)} %copy-done.20, f32[4,256,16]{1,2,0:T(8,128)S(1)} %copy-done.30, pred[256,256]{1,0:T(8,128)(4,1)S(1)} %copy-done.28, f32[4,256,16,64]{1,3,2,0:T(8,128)S(1)} %copy-done.4, f32[4,256,16]{1,2,0:T(8,128)S(1)} %bitcast.318, f32[16]{0:T(128)S(1)} %copy-done.57), kind=kOutput, calls=%fused_computation.25 | convolution fusion | flops 3240099840 | bytes 9633856 | tf_op jit(solution)/shard_map/vmap(cijh,cjhp->cihp)/dot_general | solution.py:34
  144.3 10.0 fusion.31
  170.1 12.6 %multiply_reduce_fusion.8 = (f32[1024]{0:T(1024)S(1)}, f32[1024,1024]{1,0:T(8,128)}, f32[1024,1024]{1,0:T(8,128)}) fusion(f32[1024,1024]{1,0:T(8,128)} %reshape.750, bf16[1024,2048]{1,0:T(8,128)(2,1)} %all-gather.3.cloned.1.call-done, bf16[2048,1024]{1,0:T(8,128)(2,1)} %param.25), kind=kOutput, calls=%fused_computation.79 | convolution fusion | flops 4302306304 | bytes 20975616 | tf_op jit(solution)/shard_map/dot_general | solution.py:123
  188.6 11.9 %multiply_reduce_fusion = (f32[1024]{0:T(1024)}, f32[1024]{0:T(1024)S(1)}, f32[1024,1024]{1,0:T(8,128)}) fusion(f32[1024,1024]{1,0:T(8,128)} %get-tuple-element.489, f32[1024]{0:T(1024)S(1)} %get-tuple-element.487, f32[1024]{0:T(1024)S(1)} %copy-done.22, bf16[1024,2048]{1,0:T(8,128)(2,1)} %all-gather.5.cloned.1.call-done, bf16[1024,2048]{1,0:T(8,128)(2,1)} %param.37), kind=kOutput, calls=%fused_computation.69 | convolution fusion | flops 4301256704 | bytes 16793600 | tf_op jit(solution)/shard_map/dot_general | solution.py:87
  206.6 9.2 fusion.28
  242.3 28.4 %fusion.11 = (f32[4,256,16]{1,2,0:T(8,128)S(1)}, f32[4,256,16]{1,2,0:T(8,128)}, f32[4,256,256]{2,1,0:T(8,128)}) fusion(f32[4,256,16]{1,2,0:T(8,128)S(1)} %copy-done.31, f32[4,256,256]{2,1,0:T(8,128)} %fusion.132, pred[256,256]{1,0:T(8,128)(4,1)S(1)} %copy-done.29, f32[4,256,16,64]{1,3,2,0:T(8,128)} %copy.274, f32[4,256,16]{1,2,0:T(8,128)S(1)} %bitcast.319, ...), kind=kOutput, calls=%fused_computation.27 | convolution fusion | flops 3269165056 | bytes 10813504 | tf_op jit(solution)/shard_map/transpose(jvp(vmap(cijh,cjhp->cihp)))/dot_general | solution.py:34
  284.6 9.2 while.49
  300.9 21.0 %fusion.29 = (f32[4,256,16]{1,2,0:T(8,128)S(1)}, f32[4,256,16]{1,2,0:T(8,128)}, f32[1,4,256,16,64]{2,4,3,1,0:T(8,128)}, f32[1,4,256,16,64]{2,4,3,1,0:T(8,128)}) fusion(f32[4,16,64,256]{3,2,1,0:T(8,128)S(1)} %fusion.56, f32[1,4,256,16,64]{2,4,3,1,0:T(8,128)S(1)} %copy-done.8, f32[4,256,16]{1,2,0:T(8,128)S(1)} %bitcast.320, f32[16]{0:T(128)S(1)} %copy-done.57, ...), kind=kOutput, calls=%fused_computation.61 | convolution fusion | flops 3253698560 | bytes 35061888 | tf_op jit(solution)/shard_map/transpose(jvp(vmap(cijh,cjhp->cihp)))/dot_general | solution.py:34
  324.3 9.9 reduce-window.16
  351.6 12.2 %multiply_reduce_fusion.3 = (f32[1024]{0:T(1024)S(1)}, f32[1024]{0:T(1024)S(1)}, f32[1024]{0:T(1024)S(1)}, f32[1024]{0:T(1024)S(1)}, f32[1024]{0:T(1024)S(1)}, /*index=5*/f32[1,1024,1024]{2,1,0:T(8,128)}) fusion(f32[1,1024,1024]{2,1,0:T(8,128)} %bitcast.295, f32[1024,1024]{1,0:T(8,128)} %copy-done.2, f32[1,1024,1024]{2,1,0:T(8,128)} %get-tuple-element.493, ...), kind=kLoop, calls=%fused_computation.72 | loop fusion | flops 19917824 | bytes 20996096 | tf_op jit(solution)/shard_map/transpose(jvp(vmap()))/reduce_sum | solution.py:17
  418.8 13.0 %fusion.119 = f32[1024,2048]{1,0:T(8,128)} fusion(bf16[1024,2048]{1,0:T(8,128)(2,1)} %param.37, f32[1024,1024]{1,0:T(8,128)} %get-tuple-element.489, f32[1024]{0:T(1024)S(1)} %copy-done.22, f32[1024]{0:T(1024)S(1)} %get-tuple-element.487), kind=kOutput, calls=%fused_computation.208 | convolution fusion | flops 4298113024 | bytes 16785408 | tf_op jit(solution)/shard_map/dot_general | solution.py:159
  441.8 10.4 fusion.80
  457.8 42.1 %all-reduce.25 = (bf16[1024,256]{1,0:T(8,128)(2,1)S(1)}, f32[4,256]{1,0:T(4,128)S(1)}, f32[256]{0:T(256)S(1)}) all-reduce(f32[1024,256]{1,0:T(8,128)S(1)} %fusion.95, f32[4,256]{1,0:T(4,128)S(1)} %pad_add_fusion.7, f32[256]{0:T(256)S(1)} %get-tuple-element.429), channel_id=1, replica_groups=mesh['dp'=8,'head'=4] {'head'}, use_global_device_ids=true, to_apply=%region_25.26 | all-reduce | flops 263424 | bytes 1583104 | tf_op jit(solution)/shard_map/psum | solution.py:186
  505.3 11.4 fusion.118
  516.7 11.4 fusion.135
  528.5 10.6 fusion.136
  540.1 38.0 %all-reduce.22 = (f32[4,1024]{1,0:T(4,128)}, f32[1024]{0:T(1024)}, f32[4,256]{1,0:T(4,128)}, f32[256]{0:T(256)}, f32[16]{0:T(128)}, /*index=5*/f32[16]{0:T(128)}, f32[16]{0:T(128)}, f32[1024]{0:T(1024)}) all-reduce(f32[4,1024]{1,0:T(4,128)S(1)} %pad_add_fusion.6, ...), channel_id=1, replica_groups=mesh['dp'=8,'head'=4] {'dp'}, use_global_device_ids=true, to_apply=%region_37.38 | all-reduce | flops 7472 | bytes 59776 | tf_op jit(solution)/shard_map/psum | solution.py:226
  581.9 36.9 %psum.101 = f32[2048]{0:T(1024)} all-reduce(f32[2048]{0:T(1024)S(1)} %get-tuple-element.424), channel_id=1, replica_groups=mesh['dp'=8,'head'=4] {'dp','head'}, use_global_device_ids=true, to_apply=%region_28.29 | all-reduce | flops 2048 | bytes 16384 | tf_op jit(solution)/shard_map/psum | solution.py:216
  623.5 24.9 %reduce-scatter.18.cloned.1.call-done = f32[256,16]{0,1:T(8,128)} async-done(((f32[2048,16]{0,1:T(8,128)}), f32[256,16]{0,1:T(8,128)}) %reduce-scatter.18.cloned.1.call-update) | async-done | bytes 16400 | tf_op jit(solution)/shard_map/reduce_scatter | solution.py:243
  648.4 70.9 %reduce-scatter.16.cloned.1.call-done = f32[256,256]{1,0:T(8,128)} async-done(((f32[2048,256]{1,0:T(8,128)}), f32[256,256]{1,0:T(8,128)}) %reduce-scatter.16.cloned.1.call-update) | async-done | bytes 262160 | tf_op jit(solution)/shard_map/reduce_scatter | solution.py:242
  719.3 152.6 %reduce-scatter.20.cloned.1.call-done = f32[1024,256]{1,0:T(8,128)} async-done(((f32[1024,2048]{1,0:T(8,128)}), f32[1024,256]{1,0:T(8,128)}) %reduce-scatter.20.cloned.1.call-update) | async-done | bytes 1048592 | tf_op jit(solution)/shard_map/reduce_scatter | solution.py:244
  871.9 152.7 %reduce-scatter.12.cloned.1.call-done = f32[256,1024]{1,0:T(8,128)} async-done(((f32[2048,1024]{1,0:T(8,128)}), f32[256,1024]{1,0:T(8,128)}) %reduce-scatter.12.cloned.1.call-update) | async-done | bytes 1048592 | tf_op jit(solution)/shard_map/reduce_scatter | solution.py:240
  1024.6 152.2 %reduce-scatter.14.cloned.1.call-done = f32[256,1024]{1,0:T(8,128)} async-done(((f32[2048,1024]{1,0:T(8,128)}), f32[256,1024]{1,0:T(8,128)}) %reduce-scatter.14.cloned.1.call-update) | async-done | bytes 1048592 | tf_op jit(solution)/shard_map/reduce_scatter | solution.py:241
  (322 shorter events, 287.0 us)
Async XLA Ops:
  7.2 50.8 %copy-start = (bf16[2048,256]{1,0:T(8,128)(2,1)S(1)}, bf16[2048,256]{1,0:T(8,128)(2,1)}, u32[]{:S(2)}) copy-start(bf16[2048,256]{1,0:T(8,128)(2,1)} %param.27) | copy-start | bytes 3145732
  7.2 42.1 %copy-start.24 = (bf16[2048,16]{0,1:T(8,128)(2,1)S(1)}, bf16[2048,16]{0,1:T(8,128)(2,1)}, u32[]{:S(2)}) copy-start(bf16[2048,16]{0,1:T(8,128)(2,1)} %param.28) | copy-start | bytes 196612
  7.2 42.1 %copy-start.62 = (f32[16]{0:T(128)S(1)}, f32[16]{0:T(128)}, u32[]{:S(2)}) copy-start(f32[16]{0:T(128)} %param.33) | copy-start | bytes 196
  7.3 42.1 %all-gather.3.cloned.1.call-start = ((), (), s32[]{:S(2)}) async-start(), calls=%async_computation.7 | async-start | bytes 5242880 | tf_op jit(solution)/shard_map/all_gather | solution.py:120
  12.0 176.6 %all-gather.5.cloned.1.call-start = ((), (), s32[]{:S(2)}) async-start(), calls=%async_computation.9 | async-start | bytes 5242880 | tf_op jit(solution)/shard_map/all_gather | solution.py:165
  12.7 565.4 %reduce-scatter.10.cloned.1.call-start = ((), (), s32[]{:S(2)}) async-start(), calls=%async_computation.10 | async-start | bytes 10485760 | tf_op jit(solution)/shard_map/reduce_scatter | solution.py:193
  14.1 39.2 %copy-start.63 = (f32[16]{0:T(128)}, f32[16]{0:T(128)S(1)}, u32[]{:S(2)}) copy-start(f32[16]{0:T(128)S(1)} %exponential_negate_fusion) | copy-start | bytes 196
  14.6 47.5 %copy-start.48 = (f32[1,256]{1,0:T(1,128)}, f32[1,256]{1,0:T(1,128)S(1)}, u32[]{:S(2)}) copy-start(f32[1,256]{1,0:T(1,128)S(1)} %get-tuple-element.518) | copy-start | bytes 3076
  14.6 47.5 %copy-start.50 = (f32[1,256]{1,0:T(1,128)}, f32[1,256]{1,0:T(1,128)S(1)}, u32[]{:S(2)}) copy-start(f32[1,256]{1,0:T(1,128)S(1)} %get-tuple-element.519) | copy-start | bytes 3076
  14.6 47.5 %copy-start.52 = (f32[1,256]{1,0:T(1,128)}, f32[1,256]{1,0:T(1,128)S(1)}, u32[]{:S(2)}) copy-start(f32[1,256]{1,0:T(1,128)S(1)} %get-tuple-element.520) | copy-start | bytes 3076
  14.6 47.5 %copy-start.54 = (f32[1,256]{1,0:T(1,128)}, f32[1,256]{1,0:T(1,128)S(1)}, u32[]{:S(2)}) copy-start(f32[1,256]{1,0:T(1,128)S(1)} %get-tuple-element.521) | copy-start | bytes 3076
  15.4 55.8 %copy-start.32 = (f32[1,1024]{1,0:T(1,128)}, f32[1,1024]{1,0:T(1,128)S(1)}, u32[]{:S(2)}) copy-start(f32[1,1024]{1,0:T(1,128)S(1)} %get-tuple-element.514) | copy-start | bytes 12292
  15.4 55.8 %copy-start.34 = (f32[1,1024]{1,0:T(1,128)}, f32[1,1024]{1,0:T(1,128)S(1)}, u32[]{:S(2)}) copy-start(f32[1,1024]{1,0:T(1,128)S(1)} %get-tuple-element.515) | copy-start | bytes 12292
  15.4 55.8 %copy-start.36 = (f32[1,1024]{1,0:T(1,128)}, f32[1,1024]{1,0:T(1,128)S(1)}, u32[]{:S(2)}) copy-start(f32[1,1024]{1,0:T(1,128)S(1)} %get-tuple-element.516) | copy-start | bytes 12292
  15.4 55.8 %copy-start.38 = (f32[1,1024]{1,0:T(1,128)}, f32[1,1024]{1,0:T(1,128)S(1)}, u32[]{:S(2)}) copy-start(f32[1,1024]{1,0:T(1,128)S(1)} %get-tuple-element.517) | copy-start | bytes 12292
  418.6 200.3 %reduce-scatter.8.cloned.1.call-start = ((), (), s32[]{:S(2)}) async-start(), calls=%async_computation.8 | async-start | bytes 10485760 | tf_op jit(solution)/shard_map/reduce_scatter | solution.py:158
  431.8 216.6 %reduce-scatter.18.cloned.1.call-start = ((), (), s32[]{:S(2)}) async-start(), calls=%async_computation.14 | async-start | bytes 147456 | tf_op jit(solution)/shard_map/reduce_scatter | solution.py:243
  457.7 261.6 %reduce-scatter.16.cloned.1.call-start = ((), (), s32[]{:S(2)}) async-start(), calls=%async_computation.13 | async-start | bytes 2359296 | tf_op jit(solution)/shard_map/reduce_scatter | solution.py:242
  505.0 366.9 %reduce-scatter.20.cloned.1.call-start = ((), (), s32[]{:S(2)}) async-start(), calls=%async_computation.15 | async-start | bytes 9437184 | tf_op jit(solution)/shard_map/reduce_scatter | solution.py:244
  516.7 507.9 %reduce-scatter.12.cloned.1.call-start = ((), (), s32[]{:S(2)}) async-start(), calls=%async_computation.11 | async-start | bytes 9437184 | tf_op jit(solution)/shard_map/reduce_scatter | solution.py:240
  528.2 648.6 %reduce-scatter.14.cloned.1.call-start = ((), (), s32[]{:S(2)}) async-start(), calls=%async_computation.12 | async-start | bytes 9437184 | tf_op jit(solution)/shard_map/reduce_scatter | solution.py:241
  539.2 39.0 %copy-start.7 = (bf16[256,2048]{1,0:T(8,128)(2,1)S(1)}, bf16[256,2048]{1,0:T(8,128)(2,1)}, u32[]{:S(2)}) copy-start(bf16[256,2048]{1,0:T(8,128)(2,1)} %param.23) | copy-start | bytes 3145732
  539.2 79.6 %copy-start.14 = (bf16[256,2048]{1,0:T(8,128)(2,1)S(1)}, bf16[256,2048]{1,0:T(8,128)(2,1)}, u32[]{:S(2)}) copy-start(bf16[256,2048]{1,0:T(8,128)(2,1)} %param.38) | copy-start | bytes 3145732
  539.2 79.6 %copy-start.58 = (f32[256]{0:T(256)S(1)}, f32[256]{0:T(256)}, u32[]{:S(2)}) copy-start(f32[256]{0:T(256)} %get-tuple-element.522) | copy-start | bytes 3076
  (60 other events, 539.7 us)
Sparse Core Ops, SparseCore 0:
  12.1 37.1 all-gather.2
  50.9 34.4 all-gather.4
  418.7 90.2 reduce-scatter.9
  511.6 71.7 reduce-scatter.7
  587.1 61.2 reduce-scatter.17
  652.4 66.9 reduce-scatter.15
  723.5 148.3 reduce-scatter.19
  876.5 148.0 reduce-scatter.11
  1028.8 147.9 reduce-scatter.13
where the time goes:
time: 1200 us; the launch traced here: 1180 us
  waiting for transfers between devices  588 us (49%)
  matrix products  238 us (20%)
  blocking collectives  129 us (11%)
  local copies, waits for them, and re-layouts  109 us (9%)
  other arithmetic  102 us (8%)
  between operations  16.2 us (1%)
    reduce_scatter x1, waiting for transfers between devices, per_device(): lax.psum_scatter(gate_part, 'dp', scatter_dimension=0, tiled=True)  153 us
    reduce_scatter x1, waiting for transfers between devices, per_device(): lax.psum_scatter(out_proj_part, 'dp', scatter_dimension=1, tiled=True)  153 us
    reduce_scatter x1, waiting for transfers between devices, per_device(): lax.psum_scatter(value_part, 'dp', scatter_dimension=0, tiled=True)  152 us
    reduce_scatter x1, waiting for transfers between devices, per_device(): lax.psum_scatter(state_part, 'dp', scatter_dimension=0, tiled=True)  70.9 us
    dot_general x3, matrix products, state_space(): within = jnp.einsum('cijh,cjhp->cihp', mixing, scaled, precision=HIGH)  69.8 us
    psum x1, blocking collectives, per_device(): lax.psum((d_state_pre, g_conv_state, g_conv_state_bias), 'head')  42.1 us
    dot_general x5, matrix products, contract_rows(): lax.dot_general(left, right, (((0,), (0,)), ((), ())), preferred_element_...  39.8 us
    psum x1, blocking collectives, per_device(): lax.psum((g_conv_value, g_conv_value_bias, g_step_bias, g_decay_log, g_sk...  38 us
  transfers between devices with their start and end apart: 9, of which 6 were waited for; matrix products, arithmetic and copies ran while one was open for 18% of the time, Pallas kernels for 0%

commit v1 on v0

--- a/solution.py
+++ b/solution.py
@@ -117,7 +117,15 @@
     resid = hidden_in.astype(jnp.float32)
     in_scale = lax.rsqrt(jnp.mean(resid * resid, axis=-1, keepdims=True) + EPS)
     normed = (resid * in_scale * in_gain).astype(jnp.bfloat16)
-    whole = lax.all_gather(normed, "head", axis=0, tiled=True)
+    ways, here, step = (lax.axis_size("head"), lax.axis_index("head"), normed.shape[0])
+    line, have = (normed, 1)
+    while have < ways:
+        line = jnp.concatenate(
+            [line, lax.ppermute(line, "head", [(d, (d - have) % ways) for d in range(ways)])],
+            axis=0,
+        )
+        have = 2 * have
+    whole = jnp.roll(line, here * step, axis=0)
     rows_all = whole.shape[0]
     seq_len = rows_all // seqs
     gate_pre = jnp.dot(whole, gate_proj, preferred_element_type=jnp.float32)

time: 1200 us -> 1250 us (1.042)
  waiting for transfers between devices: 588 us -> 628 us
  local copies, waits for them, and re-layouts: 109 us -> 130 us
    ppermute x0 -> x2, waiting for transfers between devices: none -> 78.7 us  [per_device(): lax.ppermute(line, 'head', [(d, (d - have) % ways) for d in range(ways)])]
    all_gather x1 -> x0, waiting for transfers between devices: 33.9 us -> none  [per_device(): whole = lax.all_gather(normed, 'head', axis=0, tiled=True)]
  transfers between devices with their start and end apart: 9 -> 10, of which waited for: 6 -> 7; matrix products, arithmetic and copies ran while one was open for 18% -> 19% of each run, Pallas kernels for 0% -> 0%
where the time goes in v1:
time: 1250 us; the launch traced here: 1240 us
  waiting for transfers between devices  628 us (50%)
  matrix products  235 us (19%)
  local copies, waits for them, and re-layouts  130 us (10%)
  blocking collectives  129 us (10%)
  other arithmetic  101 us (8%)
  between operations  16.5 us (1%)
    reduce_scatter x1, waiting for transfers between devices, per_device(): lax.psum_scatter(gate_part, 'dp', scatter_dimension=0, tiled=True)  153 us
    reduce_scatter x1, waiting for transfers between devices, per_device(): lax.psum_scatter(out_proj_part, 'dp', scatter_dimension=1, tiled=True)  153 us
    reduce_scatter x1, waiting for transfers between devices, per_device(): lax.psum_scatter(value_part, 'dp', scatter_dimension=0, tiled=True)  152 us
    ppermute x2, waiting for transfers between devices, per_device(): lax.ppermute(line, 'head', [(d, (d - have) % ways) for d in range(ways)])  78.7 us
    reduce_scatter x1, waiting for transfers between devices, per_device(): lax.psum_scatter(state_part, 'dp', scatter_dimension=0, tiled=True)  70.8 us
    dot_general x3, matrix products, state_space(): within = jnp.einsum('cijh,cjhp->cihp', mixing, scaled, precision=HIGH)  70.4 us
    psum x1, blocking collectives, per_device(): lax.psum((d_state_pre, g_conv_state, g_conv_state_bias), 'head')  42.6 us
    dot_general x5, matrix products, contract_rows(): lax.dot_general(left, right, (((0,), (0,)), ((), ())), preferred_element_...  38.3 us
  transfers between devices with their start and end apart: 10, of which 7 were waited for; matrix products, arithmetic and copies ran while one was open for 19% of the time, Pallas kernels for 0%

profile of v1, /device:TPU:0, one launch (start us, length us, event | category | flops | bytes accessed | tf_op | source)
XLA Modules:
  0.0 1243.1 jit_solution(5880778794831494170)
XLA Ops:
  14.4 12.3 collective-permute-done
  33.2 66.4 %collective-permute-done.1 = bf16[512,2048]{1,0:T(8,128)(2,1)} collective-permute-done((bf16[512,2048]{1,0:T(8,128)(2,1)}, bf16[512,2048]{1,0:T(8,128)(2,1)}, u32[]{:S(2)}, u32[]{:S(2)}) %collective-permute-start.1) | collective-permute-done | bytes 2097184 | tf_op jit(solution)/shard_map/ppermute | solution.py:124
  184.1 21.2 %fusion.9 = f32[4,16,64,256]{3,2,1,0:T(8,128)S(1)} fusion(f32[4,256,256]{2,1,0:T(8,128)S(1)} %fusion.153, f32[4,256,16]{1,2,0:T(8,128)S(1)} %get-tuple-element.534, pred[256,256]{1,0:T(8,128)(4,1)} %iota_compare_fusion, f32[4,256,16,64]{1,3,2,0:T(8,128)} %copy.274, f32[4,256,16]{1,2,0:T(8,128)S(1)} %bitcast.311, f32[16]{0:T(128)S(1)} %compare_convert_fusion), kind=kOutput, calls=%fused_computation.25 | convolution fusion | flops 3240099840 | bytes 9633856 | tf_op jit(solution)/shard_map/vmap(cijh,cjhp->cihp)/dot_general | solution.py:34
  228.9 12.7 %multiply_reduce_fusion.8 = (f32[1024]{0:T(1024)S(1)}, f32[1024,1024]{1,0:T(8,128)}, f32[1024,1024]{1,0:T(8,128)}) fusion(f32[1024,1024]{1,0:T(8,128)} %reshape.750, bf16[2048,1024]{1,0:T(8,128)(2,1)} %param.25, bf16[2048,2048]{1,0:T(8,128)(2,1)} %constant_dynamic-update-slice_fusion.2, s32[]{:T(128)S(6)} %select_n.81), kind=kOutput, calls=%fused_computation.79 | convolution fusion | flops 4302306304 | bytes 20975620 | tf_op jit(solution)/shard_map/dot_general | solution.py:131
  249.0 10.4 while.48
  259.4 11.9 multiply_reduce_fusion
  276.9 9.7 fusion.28
  303.3 29.0 %fusion.11 = (f32[4,256,16]{1,2,0:T(8,128)S(1)}, f32[4,256,16]{1,2,0:T(8,128)S(1)}, f32[4,256,256]{2,1,0:T(8,128)}) fusion(f32[4,256,16]{1,2,0:T(8,128)} %copy-done.36, f32[4,256,256]{2,1,0:T(8,128)S(1)} %copy-done.28, pred[256,256]{1,0:T(8,128)(4,1)} %iota_compare_fusion, f32[4,256,16,64]{1,3,2,0:T(8,128)} %copy.274, f32[4,256,16]{1,2,0:T(8,128)S(1)} %bitcast.312, ...), kind=kOutput, calls=%fused_computation.27 | convolution fusion | flops 3269165056 | bytes 10813504 | tf_op jit(solution)/shard_map/transpose(jvp(vmap(cijh,cjhp->cihp)))/dot_general | solution.py:34
  344.9 11.8 while.49
  362.3 20.3 %fusion.29 = (f32[4,256,16]{1,2,0:T(8,128)S(1)}, f32[4,256,16]{1,2,0:T(8,128)S(1)}, f32[1,4,256,16,64]{2,4,3,1,0:T(8,128)}, f32[1,4,256,16,64]{2,4,3,1,0:T(8,128)}) fusion(f32[4,16,64,256]{3,2,1,0:T(8,128)S(1)} %fusion.56, f32[1,4,256,16,64]{2,4,3,1,0:T(8,128)S(1)} %copy-done.7, f32[4,256,16]{1,2,0:T(8,128)S(1)} %bitcast.313, f32[16]{0:T(128)S(1)} %copy-done.64, ...), kind=kOutput, calls=%fused_computation.61 | convolution fusion | flops 3253698560 | bytes 35061888 | tf_op jit(solution)/shard_map/transpose(jvp(vmap(cijh,cjhp->cihp)))/dot_general | solution.py:34
  383.5 9.9 reduce-window.16
  409.8 12.1 multiply_reduce_fusion.3
  477.5 13.0 %fusion.141 = f32[1024,2048]{1,0:T(8,128)} fusion(bf16[1024,2048]{1,0:T(8,128)(2,1)} %param.37, f32[1024,1024]{1,0:T(8,128)} %get-tuple-element.489, f32[1024]{0:T(1024)S(1)} %copy-done.30, f32[1024]{0:T(1024)S(1)} %get-tuple-element.487), kind=kOutput, calls=%fused_computation.237 | convolution fusion | flops 4298113024 | bytes 16785408 | tf_op jit(solution)/shard_map/dot_general | solution.py:167
  518.6 42.6 %all-reduce.25 = (bf16[1024,256]{1,0:T(8,128)(2,1)S(1)}, f32[4,256]{1,0:T(4,128)S(1)}, f32[256]{0:T(256)S(1)}) all-reduce(f32[1024,256]{1,0:T(8,128)S(1)} %fusion.95, f32[4,256]{1,0:T(4,128)S(1)} %pad_add_fusion.7, f32[256]{0:T(256)S(1)} %get-tuple-element.429), channel_id=1, replica_groups=mesh['dp'=8,'head'=4] {'head'}, use_global_device_ids=true, to_apply=%region_25.26 | all-reduce | flops 263424 | bytes 1583104 | tf_op jit(solution)/shard_map/psum | solution.py:194
  566.7 12.4 fusion.140
  581.1 9.9 fusion.105
  592.6 9.6 fusion.103
  603.1 38.0 %all-reduce.22 = (f32[4,1024]{1,0:T(4,128)}, f32[1024]{0:T(1024)}, f32[4,256]{1,0:T(4,128)}, f32[256]{0:T(256)}, f32[16]{0:T(128)}, /*index=5*/f32[16]{0:T(128)}, f32[16]{0:T(128)}, f32[1024]{0:T(1024)}) all-reduce(f32[4,1024]{1,0:T(4,128)S(1)} %pad_add_fusion.6, ...), channel_id=1, replica_groups=mesh['dp'=8,'head'=4] {'dp'}, use_global_device_ids=true, to_apply=%region_37.38 | all-reduce | flops 7472 | bytes 59776 | tf_op jit(solution)/shard_map/psum | solution.py:234
  645.0 36.9 %psum.101 = f32[2048]{0:T(1024)} all-reduce(f32[2048]{0:T(1024)S(1)} %get-tuple-element.424), channel_id=1, replica_groups=mesh['dp'=8,'head'=4] {'dp','head'}, use_global_device_ids=true, to_apply=%region_28.29 | all-reduce | flops 2048 | bytes 16384 | tf_op jit(solution)/shard_map/psum | solution.py:224
  686.6 20.9 %reduce-scatter.18.cloned.1.call-done = f32[256,16]{0,1:T(8,128)} async-done(((f32[2048,16]{0,1:T(8,128)}), f32[256,16]{0,1:T(8,128)}) %reduce-scatter.18.cloned.1.call-update) | async-done | bytes 16400 | tf_op jit(solution)/shard_map/reduce_scatter | solution.py:251
  707.5 70.8 %reduce-scatter.16.cloned.1.call-done = f32[256,256]{1,0:T(8,128)} async-done(((f32[2048,256]{1,0:T(8,128)}), f32[256,256]{1,0:T(8,128)}) %reduce-scatter.16.cloned.1.call-update) | async-done | bytes 262160 | tf_op jit(solution)/shard_map/reduce_scatter | solution.py:250
  778.3 152.5 %reduce-scatter.20.cloned.1.call-done = f32[1024,256]{1,0:T(8,128)} async-done(((f32[1024,2048]{1,0:T(8,128)}), f32[1024,256]{1,0:T(8,128)}) %reduce-scatter.20.cloned.1.call-update) | async-done | bytes 1048592 | tf_op jit(solution)/shard_map/reduce_scatter | solution.py:252
  930.9 152.7 %reduce-scatter.12.cloned.1.call-done = f32[256,1024]{1,0:T(8,128)} async-done(((f32[2048,1024]{1,0:T(8,128)}), f32[256,1024]{1,0:T(8,128)}) %reduce-scatter.12.cloned.1.call-update) | async-done | bytes 1048592 | tf_op jit(solution)/shard_map/reduce_scatter | solution.py:248
  1083.5 152.3 %reduce-scatter.14.cloned.1.call-done = f32[256,1024]{1,0:T(8,128)} async-done(((f32[2048,1024]{1,0:T(8,128)}), f32[256,1024]{1,0:T(8,128)}) %reduce-scatter.14.cloned.1.call-update) | async-done | bytes 1048592 | tf_op jit(solution)/shard_map/reduce_scatter | solution.py:249
  (348 shorter events, 317.5 us)
Async XLA Ops:
  7.2 135.8 %copy-start = (bf16[2048,256]{1,0:T(8,128)(2,1)S(1)}, bf16[2048,256]{1,0:T(8,128)(2,1)}, u32[]{:S(2)}) copy-start(bf16[2048,256]{1,0:T(8,128)(2,1)} %param.27) | copy-start | bytes 3145732
  7.2 252.2 %all-gather.2.cloned.1.call-start = ((), (), s32[]{:S(2)}) async-start(), calls=%async_computation.8 | async-start | bytes 5242880 | tf_op jit(solution)/shard_map/all_gather | solution.py:173
  12.0 14.7 %collective-permute-start = (bf16[256,2048]{1,0:T(8,128)(2,1)S(1)}, bf16[256,2048]{1,0:T(8,128)(2,1)S(1)}, u32[]{:S(2)}, u32[]{:S(2)}) collective-permute-start(bf16[256,2048]{1,0:T(8,128)(2,1)S(1)} %get-tuple-element.497), channel_id=1, source_target_pairs={{0,3},{1,0},{2,1},{3,2},{4,7},{5,4},{6,5},{7,6},{8,11},{9,8},{10,9... | collective-permute-start | bytes 3145736 | tf_op jit(solution)/shard_map/ppermute | solution.py:124
  28.4 71.2 %collective-permute-start.1 = (bf16[512,2048]{1,0:T(8,128)(2,1)}, bf16[512,2048]{1,0:T(8,128)(2,1)}, u32[]{:S(2)}, u32[]{:S(2)}) collective-permute-start(bf16[512,2048]{1,0:T(8,128)(2,1)} %pad_maximum_fusion), channel_id=1, source_target_pairs={{0,2},{1,3},{2,0},{3,1},{4,6},{5,7},{6,4},{7,5},{8,10},{9,11},{10,... | collective-permute-start | bytes 6291464 | tf_op jit(solution)/shard_map/ppermute | solution.py:124
  29.0 612.2 %reduce-scatter.10.cloned.1.call-start = ((), (), s32[]{:S(2)}) async-start(), calls=%async_computation.9 | async-start | bytes 10485760 | tf_op jit(solution)/shard_map/reduce_scatter | solution.py:201
  29.8 175.5 %copy-start.63 = (f32[16]{0:T(128)}, f32[16]{0:T(128)S(1)}, u32[]{:S(2)}) copy-start(f32[16]{0:T(128)S(1)} %compare_convert_fusion) | copy-start | bytes 196
  30.6 81.4 %copy-start.70 = (f32[16]{0:T(128)}, f32[16]{0:T(128)S(1)}, u32[]{:S(2)}) copy-start(f32[16]{0:T(128)S(1)} %exponential_negate_fusion) | copy-start | bytes 196
  30.6 115.9 %copy-start.55 = (f32[1,256]{1,0:T(1,128)}, f32[1,256]{1,0:T(1,128)S(1)}, u32[]{:S(2)}) copy-start(f32[1,256]{1,0:T(1,128)S(1)} %get-tuple-element.520) | copy-start | bytes 3076
  30.6 115.9 %copy-start.57 = (f32[1,256]{1,0:T(1,128)}, f32[1,256]{1,0:T(1,128)S(1)}, u32[]{:S(2)}) copy-start(f32[1,256]{1,0:T(1,128)S(1)} %get-tuple-element.521) | copy-start | bytes 3076
  30.6 115.9 %copy-start.59 = (f32[1,256]{1,0:T(1,128)}, f32[1,256]{1,0:T(1,128)S(1)}, u32[]{:S(2)}) copy-start(f32[1,256]{1,0:T(1,128)S(1)} %get-tuple-element.522) | copy-start | bytes 3076
  30.6 115.9 %copy-start.61 = (f32[1,256]{1,0:T(1,128)}, f32[1,256]{1,0:T(1,128)S(1)}, u32[]{:S(2)}) copy-start(f32[1,256]{1,0:T(1,128)S(1)} %get-tuple-element.523) | copy-start | bytes 3076
  30.7 91.5 %copy-start.38 = (f32[1,1024]{1,0:T(1,128)}, f32[1,1024]{1,0:T(1,128)S(1)}, u32[]{:S(2)}) copy-start(f32[1,1024]{1,0:T(1,128)S(1)} %get-tuple-element.516) | copy-start | bytes 12292
  30.7 91.5 %copy-start.40 = (f32[1,1024]{1,0:T(1,128)}, f32[1,1024]{1,0:T(1,128)S(1)}, u32[]{:S(2)}) copy-start(f32[1,1024]{1,0:T(1,128)S(1)} %get-tuple-element.517) | copy-start | bytes 12292
  30.7 91.5 %copy-start.42 = (f32[1,1024]{1,0:T(1,128)}, f32[1,1024]{1,0:T(1,128)S(1)}, u32[]{:S(2)}) copy-start(f32[1,1024]{1,0:T(1,128)S(1)} %get-tuple-element.518) | copy-start | bytes 12292
  30.7 91.5 %copy-start.44 = (f32[1,1024]{1,0:T(1,128)}, f32[1,1024]{1,0:T(1,128)S(1)}, u32[]{:S(2)}) copy-start(f32[1,1024]{1,0:T(1,128)S(1)} %get-tuple-element.519) | copy-start | bytes 12292
  30.7 73.0 %copy-start.16 = (bf16[256,2048]{1,0:T(8,128)(2,1)S(1)}, bf16[256,2048]{1,0:T(8,128)(2,1)}, u32[]{:S(2)}) copy-start(bf16[256,2048]{1,0:T(8,128)(2,1)} %copy-done.15) | copy-start | bytes 3145732
  477.2 204.7 %reduce-scatter.8.cloned.1.call-start = ((), (), s32[]{:S(2)}) async-start(), calls=%async_computation.7 | async-start | bytes 10485760 | tf_op jit(solution)/shard_map/reduce_scatter | solution.py:166
  490.5 217.0 %reduce-scatter.18.cloned.1.call-start = ((), (), s32[]{:S(2)}) async-start(), calls=%async_computation.13 | async-start | bytes 147456 | tf_op jit(solution)/shard_map/reduce_scatter | solution.py:251
  518.5 259.8 %reduce-scatter.16.cloned.1.call-start = ((), (), s32[]{:S(2)}) async-start(), calls=%async_computation.12 | async-start | bytes 2359296 | tf_op jit(solution)/shard_map/reduce_scatter | solution.py:250
  566.4 364.5 %reduce-scatter.20.cloned.1.call-start = ((), (), s32[]{:S(2)}) async-start(), calls=%async_computation.14 | async-start | bytes 9437184 | tf_op jit(solution)/shard_map/reduce_scatter | solution.py:252
  579.1 504.5 %reduce-scatter.12.cloned.1.call-start = ((), (), s32[]{:S(2)}) async-start(), calls=%async_computation.10 | async-start | bytes 9437184 | tf_op jit(solution)/shard_map/reduce_scatter | solution.py:248
  591.0 644.8 %reduce-scatter.14.cloned.1.call-start = ((), (), s32[]{:S(2)}) async-start(), calls=%async_computation.11 | async-start | bytes 9437184 | tf_op jit(solution)/shard_map/reduce_scatter | solution.py:249
  602.2 79.7 %copy-start.18 = (bf16[256,2048]{1,0:T(8,128)(2,1)S(1)}, bf16[256,2048]{1,0:T(8,128)(2,1)}, u32[]{:S(2)}) copy-start(bf16[256,2048]{1,0:T(8,128)(2,1)} %param.38) | copy-start | bytes 3145732
  602.3 79.7 %copy-start.66 = (f32[256]{0:T(256)S(1)}, f32[256]{0:T(256)}, u32[]{:S(2)}) copy-start(f32[256]{0:T(256)} %get-tuple-element.524) | copy-start | bytes 3076
  (70 other events, 764.9 us)
Sparse Core Ops, SparseCore 0:
  29.1 58.4 all-gather.1
  477.4 90.5 reduce-scatter.9
  570.7 71.7 reduce-scatter.7
  646.2 61.2 reduce-scatter.17
  711.5 66.8 reduce-scatter.15
  782.4 148.4 reduce-scatter.19
  935.5 147.9 reduce-scatter.11
  1087.7 148.0 reduce-scatter.13
